TPU v7x, 512 devices: a whole 4x8x8 slice. The times are simulated.
512 devices in a mesh: grp: 16 (over x, z_hi, core), dev: 32 (over y, z_lo).
Axes of the slice: x: 4, y: 8, z: 8 (z_hi: 2, z_lo: 4; z = z_hi * 4 + z_lo), core: 2. Of those that a mesh axis runs over, the one named last changes fastest.
Arguments:
- adjoint: bfloat16 [1024, 30, 192], P(('grp', 'dev')), may hold values from -6 to 6
- jacobian_tiles: bfloat16 [1024, 17, 36864], P(('grp', 'dev'))
- columns: int32 [1024, 16], P(('grp', 'dev')), may hold values from 0 to 127, as said below
- cell_rates: float32 [1024, 192], P(('grp', 'dev')), may hold values from 0.05 to 0.5
- precond: bfloat16 [1024, 36864], P(('grp', 'dev')), may hold values from -0.4375 to 0.4375
- lower_list: int32 [16, 32], replicated, may hold values from 0 to 63, as said below
- upper_list: int32 [16, 32], replicated, may hold values from 0 to 63, as said below
Outputs:
- preconditioned: bfloat16 [1024, 30, 192], P(('grp', 'dev'))
Inputs may be any that keep to these rules, and one draw needn't show every extreme that they name: `columns`: rows of the first group name no value in 64 .. 95, rows of the last group no value of 96 or more. `lower_list`: the entries of a row are distinct. `upper_list`: the entries of a row are distinct.
All inputs are finite; a program needn't handle non-finite values.
Results may differ from a plain program's by a relative error of at most 0.005.
Values sent between devices are 32-bit elements; how exact they have to be, the bound alone decides.
No kernel may reach another device: no remote copies, remote signals or barrier semaphores. Data moves between devices by JAX's collectives and lax.ppermute only.
A program may use at most 64 MiB of HBM per device.

v0:
```python
import jax
import jax.numpy as jnp
from jax import lax
from jax.sharding import PartitionSpec as P

INST = 15
ADJ = 2


def passed_along(value, axis, by):
    length = lax.axis_size(axis)
    pairs = [(i, i + by) for i in range(length) if 0 <= i + by < length]
    return lax.ppermute(value, axis, pairs)


def spectral_matrix(length):
    row_index = jnp.arange(length)[:, None]
    col_index = jnp.arange(length)[None, :]
    offset = row_index - col_index
    parity = jnp.where(offset % 2 == 0, 1.0, -1.0).astype(jnp.float32)
    phase_angle = jnp.pi / length * offset.astype(jnp.float32)
    sine_values = jnp.where(offset == 0, 1.0, jnp.sin(phase_angle))
    return jnp.where(offset == 0, 0.0, 0.5 * parity / sine_values)


def shards(adjoint, jacobian_tiles, columns, cell_rates, precond, lower_list, upper_list):
    blocks, row_count, tile_width = adjoint.shape
    tile_slots = jacobian_tiles.shape[1]
    square_tiles = jacobian_tiles.reshape(blocks, tile_slots, tile_width, tile_width)
    square_precond = precond.reshape(blocks, tile_width, tile_width)
    members = lax.axis_size("dev")
    group_blocks = blocks * members
    groups = lower_list.shape[0]
    halo_slots = lower_list.shape[1]
    member = lax.axis_index("dev")
    group_id = lax.axis_index("grp")
    products = jnp.einsum(
        "brt,bkts->bkrs", adjoint, square_tiles, preferred_element_type=jnp.float32
    )
    flat_terms = products.reshape(blocks * tile_slots, row_count * tile_width)
    own_ids = member * blocks + jnp.arange(blocks, dtype=jnp.int32)
    targets = jnp.concatenate([own_ids[:, None], columns], axis=1).reshape(-1)
    slot_ids = group_blocks + jnp.arange(2 * halo_slots, dtype=jnp.int32)
    picker = (slot_ids[:, None] == targets[None, :]).astype(jnp.float32)
    halo_terms = jnp.dot(
        picker, flat_terms, precision=lax.Precision.HIGHEST, preferred_element_type=jnp.float32
    )
    upper_group = jnp.minimum(group_id + 1, groups - 1)
    lower_group = jnp.maximum(group_id - 1, 0)
    from_above = passed_along(halo_terms[:halo_slots], "grp", -1)
    from_below = passed_along(halo_terms[halo_slots:], "grp", 1)
    lower_ids = lax.dynamic_slice(lower_list, (upper_group, 0), (1, halo_slots))[0]
    upper_ids = lax.dynamic_slice(upper_list, (lower_group, 0), (1, halo_slots))[0]
    incoming = jnp.concatenate([from_above, from_below], axis=0)
    incoming_ids = jnp.concatenate([lower_ids, upper_ids])
    positions = jnp.arange(blocks * lax.axis_size("dev"), dtype=jnp.int32)
    own_rows = (positions[:, None] == targets[None, :]).astype(jnp.float32)
    halo_rows = (positions[:, None] == incoming_ids[None, :]).astype(jnp.float32)
    local_sum = jnp.dot(
        own_rows, flat_terms, precision=lax.Precision.HIGHEST, preferred_element_type=jnp.float32
    )
    transposed = lax.psum_scatter(
        local_sum
        + jnp.dot(
            halo_rows, incoming, precision=lax.Precision.HIGHEST, preferred_element_type=jnp.float32
        ),
        "dev",
        scatter_dimension=0,
        tiled=True,
    )
    spectral = spectral_matrix(INST)
    instances = adjoint.astype(jnp.float32).reshape(blocks, ADJ, INST, tile_width)
    spectral_part = jnp.einsum(
        "nm,bant->bamt", spectral, instances, precision=lax.Precision.HIGHEST
    )
    spectral_part = cell_rates[:, None, None, :] * spectral_part
    combined = (
        transposed.reshape(blocks, row_count, tile_width)
        + spectral_part.reshape(blocks, row_count, tile_width)
    ).astype(jnp.bfloat16)
    result = jnp.einsum(
        "brt,bts->brs", combined, square_precond, preferred_element_type=jnp.float32
    )
    return result.astype(jnp.bfloat16)


def solution(mesh):
    return jax.shard_map(
        shards,
        mesh=mesh,
        in_specs=(
            P(("grp", "dev"), None, None),
            P(("grp", "dev"), None, None),
            P(("grp", "dev"), None),
            P(("grp", "dev"), None),
            P(("grp", "dev"), None),
            P(),
            P(),
        ),
        out_specs=P(("grp", "dev"), None, None),
        check_vma=False,
    )
```

profile of v0, /device:TPU:6, one launch (start us, length us, event | category | flops | bytes accessed | tf_op | source)
XLA Modules:
  0.0 387.8 jit_solution(14558135599448934590)
XLA Ops:
  6.5 0.8 pad_add_fusion
  7.3 0.1 eq.25
  7.4 6.3 %reshape.32 = bf16[2,17,192,192]{3,2,0,1:T(8,128)(2,1)S(1)} reshape(bf16[2,17,36864]{2,0,1:T(2,128)(2,1)} %param.8) | data formatting | bytes 5013504 | tf_op jit(solution)/shard_map/reshape | solution.py:29
  13.7 1.7 fusion.5
  15.4 1.7 reshape.33
  17.1 0.8 fusion.14
  17.9 1.0 fusion.56
  18.8 10.6 %collective-permute-start = (f32[32,5760]{1,0:T(8,128)}, f32[32,5760]{1,0:T(8,128)S(1)}, u32[]{:S(2)}, u32[]{:S(2)}) collective-permute-start(f32[32,5760]{1,0:T(8,128)} %get-tuple-element.5), channel_id=1, source_target_pairs={{32,0},{64,32},{96,64},{128,96},{160,128},{192,160},{224,192},{256... | collective-permute-start | bytes 2211848 | tf_op jit(solution)/shard_map/ppermute | solution.py:13
  29.4 1.9 collective-permute-start.1
  31.4 0.7 dynamic-slice_bitcast_fusion
  32.1 0.1 pad_add_fusion.1
  32.2 0.7 fusion.13
  32.9 20.2 %collective-permute-done = f32[32,5760]{1,0:T(8,128)S(1)} collective-permute-done((f32[32,5760]{1,0:T(8,128)}, f32[32,5760]{1,0:T(8,128)S(1)}, u32[]{:S(2)}, u32[]{:S(2)}) %collective-permute-start) | collective-permute-done | bytes 737312 | tf_op jit(solution)/shard_map/ppermute | solution.py:13
  53.1 2.1 convolution_add_fusion
  55.3 0.9 copy-done.1
  56.1 0.2 reshape.37
  56.4 0.2 fusion.8
  56.6 0.1 copy.21
  56.6 1.3 dynamic-slice
  58.6 320.5 %all-reduce.3.cloned.1.call-done = f32[64,5760]{1,0:T(8,128)} async-done(((f32[64,5760]{1,0:T(8,128)}), f32[64,5760]{1,0:T(8,128)}) %all-reduce.3.cloned.1.call-update) | async-done | bytes 1474576
  379.1 0.9 constant_dynamic-slice_fusion
  380.0 0.1 reshape.34
  380.1 0.1 convolution_convert_fusion
  380.3 0.7 copy.23
  (10 shorter events, 0.0 us)
Async XLA Ops:
  6.5 7.1 %copy-start = (bf16[2,30,192]{2,0,1:T(2,128)(2,1)S(1)}, bf16[2,30,192]{2,0,1:T(2,128)(2,1)}, u32[]{:S(2)}) copy-start(bf16[2,30,192]{2,0,1:T(2,128)(2,1)} %param.7) | copy-start | bytes 69124
  6.5 372.5 %all-reduce.3.cloned.1.call-start = ((), (), s32[]{:S(2)}) async-start(), calls=%async_computation | async-start | bytes 2949120
  18.8 34.3 %collective-permute-start = (f32[32,5760]{1,0:T(8,128)}, f32[32,5760]{1,0:T(8,128)S(1)}, u32[]{:S(2)}, u32[]{:S(2)}) collective-permute-start(f32[32,5760]{1,0:T(8,128)} %get-tuple-element.5), channel_id=1, source_target_pairs={{32,0},{64,32},{96,64},{128,96},{160,128},{192,160},{224,192},{256... | collective-permute-start | bytes 2211848 | tf_op jit(solution)/shard_map/ppermute | solution.py:13
  29.4 23.7 %collective-permute-start.1 = (f32[32,5760]{1,0:T(8,128)S(1)}, f32[32,5760]{1,0:T(8,128)S(1)}, u32[]{:S(2)}, u32[]{:S(2)}) collective-permute-start(f32[32,5760]{1,0:T(8,128)S(1)} %get-tuple-element.6), channel_id=1, source_target_pairs={{0,32},{32,64},{64,96},{96,128},{128,160},{160,192},{192,224},{224... | collective-permute-start | bytes 2211848 | tf_op jit(solution)/shard_map/ppermute | solution.py:13
  55.2 0.9 copy-start.1
  55.2 1.1 copy-start.2
Sparse Core Ops, SparseCore 0:
  55.4 323.6 all-reduce.2
where the time goes:
time: 388 us
  waiting for transfers between devices  341 us (88%)
  between operations  14.2 us (4%)
  local copies, waits for them, and re-layouts  13.8 us (4%)
  starting transfers between devices  12.5 us (3%)
  matrix products  5.66 us (1%)
    unnamed x2, waiting for transfers between devices  321 us
    ppermute x2, waiting for transfers between devices, passed_along(): return lax.ppermute(value, axis, pairs)  20.2 us
    ppermute x2, starting transfers between devices, passed_along(): return lax.ppermute(value, axis, pairs)  12.5 us
  transfers between devices with their start and end apart: 3, of which 2 were waited for; matrix products, arithmetic and copies ran while one was open for 1% of the time, Pallas kernels for 0%

commit v1 on v0

--- a/solution.py
+++ b/solution.py
@@ -59,15 +59,13 @@
     local_sum = jnp.dot(
         own_rows, flat_terms, precision=lax.Precision.HIGHEST, preferred_element_type=jnp.float32
     )
-    transposed = lax.psum_scatter(
-        local_sum
-        + jnp.dot(
-            halo_rows, incoming, precision=lax.Precision.HIGHEST, preferred_element_type=jnp.float32
-        ),
-        "dev",
-        scatter_dimension=0,
-        tiled=True,
+    dense = local_sum + jnp.dot(
+        halo_rows, incoming, precision=lax.Precision.HIGHEST, preferred_element_type=jnp.float32
     )
+    shared = lax.all_to_all(
+        dense.reshape(members, blocks * row_count * tile_width), "dev", 0, 0, tiled=True
+    )
+    transposed = jnp.sum(shared, axis=0)
     spectral = spectral_matrix(INST)
     instances = adjoint.astype(jnp.float32).reshape(blocks, ADJ, INST, tile_width)
     spectral_part = jnp.einsum(

time: 388 us -> 114 us (0.29)
  waiting for transfers between devices: 341 us -> 57.1 us
  starting transfers between devices: 12.5 us -> 37 us
  between operations: 14.2 us -> 0.13 us
    unnamed x2 -> x0, waiting for transfers between devices: 321 us -> none
    all_to_all x0 -> x1, waiting for transfers between devices: none -> 37.1 us  [shards(): lax.all_to_all(dense.reshape(members, blocks * row_count * tile_width), '...]
    all_to_all x0 -> x1, starting transfers between devices: none -> 24.4 us  [shards(): lax.all_to_all(dense.reshape(members, blocks * row_count * tile_width), '...]
  transfers between devices with their start and end apart: 3 -> 3, of which waited for: 2 -> 2; matrix products, arithmetic and copies ran while one was open for 1% -> 2% of each run, Pallas kernels for 0% -> 0%
where the time goes in v1:
time: 114 us
  waiting for transfers between devices  57.1 us (50%)
  starting transfers between devices  37 us (32%)
  local copies, waits for them, and re-layouts  13.6 us (12%)
  matrix products  4.53 us (4%)
  other arithmetic  1.69 us (1%)
    all_to_all x1, waiting for transfers between devices, shards(): lax.all_to_all(dense.reshape(members, blocks * row_count * tile_width), '...  37.1 us
    all_to_all x1, starting transfers between devices, shards(): lax.all_to_all(dense.reshape(members, blocks * row_count * tile_width), '...  24.4 us
    ppermute x2, waiting for transfers between devices, passed_along(): return lax.ppermute(value, axis, pairs)  20 us
    ppermute x2, starting transfers between devices, passed_along(): return lax.ppermute(value, axis, pairs)  12.5 us
    reshape x1, local copies, waits for them, and re-layouts, shards(): jacobian_tiles.reshape(blocks, tile_slots, tile_width, tile_width)  6.28 us
    all_to_all x1, local copies, waits for them, and re-layouts, shards(): lax.all_to_all(dense.reshape(members, blocks * row_count * tile_width), '...  2.58 us
  transfers between devices with their start and end apart: 3, of which 2 were waited for; matrix products, arithmetic and copies ran while one was open for 2% of the time, Pallas kernels for 0%

profile of v1, /device:TPU:6, one launch (start us, length us, event | category | flops | bytes accessed | tf_op | source)
XLA Modules:
  0.0 113.9 jit_solution(11621123607646464606)
XLA Ops:
  0.0 0.8 pad_add_fusion
  0.8 0.1 eq.25
  0.9 6.3 %reshape.36 = bf16[2,17,192,192]{3,2,0,1:T(8,128)(2,1)S(1)} reshape(bf16[2,17,36864]{2,0,1:T(2,128)(2,1)} %param.8) | data formatting | bytes 5013504 | tf_op jit(solution)/shard_map/reshape | solution.py:29
  7.2 1.7 %fusion.5 = f32[2,17,30,192]{3,2,1,0:T(8,128)} fusion(bf16[2,17,192,192]{3,2,0,1:T(8,128)(2,1)S(1)} %reshape.36, bf16[2,30,192,1]{2,0,1,3:T(2,128)(2,1)S(1)} %bitcast.21), kind=kOutput, calls=%fused_computation.6 | convolution fusion | flops 75202560 | bytes 3313152 | tf_op jit(solution)/shard_map/brt,bkts->bkrs/dot_general | solution.py:37
  8.9 1.7 %reshape.37 = f32[34,5760]{1,0:T(8,128)S(1)} reshape(f32[2,17,30,192]{3,2,1,0:T(8,128)} %fusion.5) | data formatting | bytes 1566720 | tf_op jit(solution)/shard_map/reshape | solution.py:40
  10.6 0.8 fusion.14
  11.3 1.2 %fusion.56 = (f32[32,5760]{1,0:T(8,128)}, f32[32,5760]{1,0:T(8,128)}) fusion(f32[64,5760]{1,0:T(8,128)S(1)} %fusion.14), kind=kLoop, calls=%fused_computation.65 | loop fusion | bytes 2949120 | tf_op jit(solution)/shard_map/slice | solution.py:50
  12.6 10.6 %collective-permute-start = (f32[32,5760]{1,0:T(8,128)}, f32[32,5760]{1,0:T(8,128)S(1)}, u32[]{:S(2)}, u32[]{:S(2)}) collective-permute-start(f32[32,5760]{1,0:T(8,128)} %get-tuple-element.5), channel_id=1, source_target_pairs={{32,0},{64,32},{96,64},{128,96},{160,128},{192,160},{224,192},{256... | collective-permute-start | bytes 2211848 | tf_op jit(solution)/shard_map/ppermute | solution.py:13
  23.2 1.9 %collective-permute-start.1 = (f32[32,5760]{1,0:T(8,128)}, f32[32,5760]{1,0:T(8,128)S(1)}, u32[]{:S(2)}, u32[]{:S(2)}) collective-permute-start(f32[32,5760]{1,0:T(8,128)} %get-tuple-element.6), channel_id=1, source_target_pairs={{0,32},{32,64},{64,96},{96,128},{128,160},{160,192},{192,224},{224... | collective-permute-start | bytes 2211848 | tf_op jit(solution)/shard_map/ppermute | solution.py:13
  25.1 0.7 dynamic-slice_bitcast_fusion
  25.8 0.1 pad_add_fusion.1
  25.9 0.7 fusion.13
  26.7 20.0 %collective-permute-done = f32[32,5760]{1,0:T(8,128)S(1)} collective-permute-done((f32[32,5760]{1,0:T(8,128)}, f32[32,5760]{1,0:T(8,128)S(1)}, u32[]{:S(2)}, u32[]{:S(2)}) %collective-permute-start) | collective-permute-done | bytes 737312 | tf_op jit(solution)/shard_map/ppermute | solution.py:13
  46.7 0.9 convolution_add_fusion
  47.6 2.6 %all_to_all.8 = f32[32,1,11520]{2,1,0:T(1,128)} reshape(f32[64,5760]{1,0:T(8,128)S(1)} %convolution_add_fusion) | data formatting | bytes 2949120 | tf_op jit(solution)/shard_map/all_to_all | solution.py:65
  50.2 24.4 %all-to-all-start = ((f32[32,1,11520]{2,1,0:T(1,128)}), f32[32,1,11520]{2,1,0:T(1,128)S(1)}, u32[]{:S(2)}, u32[]{:S(2)}) async-start(f32[32,1,11520]{2,1,0:T(1,128)} %all_to_all.8), calls=%async_computation | async-start | bytes 2949120 | tf_op jit(solution)/shard_map/all_to_all | solution.py:65
  74.7 0.2 reshape.41
  74.9 0.2 fusion.8
  75.1 0.1 copy.22
  75.2 37.1 %all-to-all-done = f32[32,1,11520]{2,1,0:T(1,128)S(1)} async-done(((f32[32,1,11520]{2,1,0:T(1,128)}), f32[32,1,11520]{2,1,0:T(1,128)S(1)}, u32[]{:S(2)}, u32[]{:S(2)}) %all-to-all-start) | async-done | bytes 1474592 | tf_op jit(solution)/shard_map/all_to_all | solution.py:65
  112.2 0.8 reduce_sum.9
  113.1 0.1 reshape.38
  113.2 0.1 convolution_convert_fusion
  113.3 0.6 copy.24
  (9 shorter events, 0.0 us)
Async XLA Ops:
  0.0 7.1 %copy-start = (bf16[2,30,192]{2,0,1:T(2,128)(2,1)S(1)}, bf16[2,30,192]{2,0,1:T(2,128)(2,1)}, u32[]{:S(2)}) copy-start(bf16[2,30,192]{2,0,1:T(2,128)(2,1)} %param.7) | copy-start | bytes 69124
  12.6 34.1 %collective-permute-start = (f32[32,5760]{1,0:T(8,128)}, f32[32,5760]{1,0:T(8,128)S(1)}, u32[]{:S(2)}, u32[]{:S(2)}) collective-permute-start(f32[32,5760]{1,0:T(8,128)} %get-tuple-element.5), channel_id=1, source_target_pairs={{32,0},{64,32},{96,64},{128,96},{160,128},{192,160},{224,192},{256... | collective-permute-start | bytes 2211848 | tf_op jit(solution)/shard_map/ppermute | solution.py:13
  23.2 23.5 %collective-permute-start.1 = (f32[32,5760]{1,0:T(8,128)}, f32[32,5760]{1,0:T(8,128)S(1)}, u32[]{:S(2)}, u32[]{:S(2)}) collective-permute-start(f32[32,5760]{1,0:T(8,128)} %get-tuple-element.6), channel_id=1, source_target_pairs={{0,32},{32,64},{64,96},{96,128},{128,160},{160,192},{192,224},{224... | collective-permute-start | bytes 2211848 | tf_op jit(solution)/shard_map/ppermute | solution.py:13
  50.2 24.4 %copy-start.1 = (bf16[2,36864]{1,0:T(2,128)(2,1)S(1)}, bf16[2,36864]{1,0:T(2,128)(2,1)}, u32[]{:S(2)}) copy-start(bf16[2,36864]{1,0:T(2,128)(2,1)} %param.11) | copy-start | bytes 442372
  50.2 24.7 %copy-start.2 = (f32[2,192]{1,0:T(2,128)S(1)}, f32[2,192]{1,0:T(2,128)}, u32[]{:S(2)}) copy-start(f32[2,192]{1,0:T(2,128)} %param.10) | copy-start | bytes 4612
  50.2 62.0 %all-to-all-start = ((f32[32,1,11520]{2,1,0:T(1,128)}), f32[32,1,11520]{2,1,0:T(1,128)S(1)}, u32[]{:S(2)}, u32[]{:S(2)}) async-start(f32[32,1,11520]{2,1,0:T(1,128)} %all_to_all.8), calls=%async_computation | async-start | bytes 2949120 | tf_op jit(solution)/shard_map/all_to_all | solution.py:65
